TPU v7x, 512 devices: a whole 4x4x16 slice. The times are simulated.
512 devices in a mesh: grp: 16 (over y, x), tp: 32 (over z, core).
Axes of the slice: x: 4, y: 4, z: 16, core: 2. Of those that a mesh axis runs over, the one named last changes fastest.
Arguments:
- tokens: bfloat16 [6144, 5120], P('grp'), may hold values from -36 to 36
- trainer_panels: bfloat16 [64, 5120, 128], P('tp', 'grp'), may hold values from -0.078125 to 0.078125
- panel_home: int32 [48], replicated, may hold values from 0 to 63, as said below
- lengths: int32 [16, 4], P('grp'), may hold values from 1 to 192, 384 in all within a row
Outputs:
- context: float32 [6144, 4096], P(('grp', 'tp'))
Inputs may be any that keep to these rules, and one draw needn't show every extreme that they name: `panel_home`: entries are distinct; entry p is 2 times the tp index of the trainer device that holds panel p, plus the panel's slot on that device. Panels 0 to 31 are query heads, the next 8 key heads, the last 8 value heads. Some trainer device holds 2 panels.
All inputs are finite; a program needn't handle non-finite values.
Results may differ from a plain program's by a relative error of at most 0.012.
Values may be sent and summed in bfloat16 or wider, within the bound.
A program may use at most 64 MiB of HBM per device.

v0:
```python
import jax
import jax.numpy as jnp
from jax import lax
from jax.sharding import PartitionSpec as P


def on_device(tokens, trainer_panels, panel_home, lengths):
    tp_count = lax.axis_size("tp")
    member_id = lax.axis_index("tp")
    kv_count = (panel_home.shape[0] - tp_count) // 2
    group_size = tp_count // kv_count
    slot_count = trainer_panels.shape[0]
    head_dim = trainer_panels.shape[2]
    needed = jnp.stack(
        [
            member_id,
            tp_count + member_id // group_size,
            tp_count + kv_count + member_id // group_size,
        ]
    )
    wanted = panel_home[needed]
    peer_ids = jnp.arange(tp_count, dtype=jnp.int32)
    reader_need = jnp.stack(
        [peer_ids, tp_count + peer_ids // group_size, tp_count + kv_count + peer_ids // group_size],
        axis=1,
    )
    reader_home = panel_home[reader_need]
    local_slot = reader_home - member_id * slot_count
    owned_here = (local_slot >= 0) & (local_slot < slot_count)
    picked = trainer_panels[jnp.clip(local_slot, 0, slot_count - 1)]
    outbound = jnp.where(owned_here[:, :, None, None], picked, jnp.zeros_like(picked))
    arrived = lax.all_to_all(outbound, "tp", split_axis=0, concat_axis=0, tiled=True)
    source = wanted // slot_count
    selected = jnp.stack([arrived[source[need_pos], need_pos] for need_pos in range(3)], axis=1)
    full_panels = lax.all_gather(selected, "grp", axis=0, tiled=True)
    weights = full_panels.reshape(full_panels.shape[0], 3 * head_dim)
    projected = jnp.dot(tokens, weights, preferred_element_type=jnp.float32).astype(jnp.bfloat16)
    query_rows = projected[:, :head_dim]
    key_rows = projected[:, head_dim : 2 * head_dim]
    value_rows = projected[:, 2 * head_dim :]
    seq_total = query_rows.shape[0]
    position = jnp.arange(seq_total, dtype=jnp.int32)
    bounds = jnp.cumsum(lengths[0])
    segment = jnp.sum((position[:, None] >= bounds[None, :]).astype(jnp.int32), axis=1)
    allowed = (segment[:, None] == segment[None, :]) & (position[None, :] <= position[:, None])
    score_scale = head_dim ** (-0.5)
    scores = (
        lax.dot_general(
            query_rows, key_rows, (((1,), (1,)), ((), ())), preferred_element_type=jnp.float32
        )
        * score_scale
    )
    masked = jnp.where(allowed, scores, -jnp.inf)
    row_peak = jnp.max(masked, axis=1, keepdims=True)
    row_exp = jnp.exp(masked - row_peak)
    attn_probs = (row_exp / jnp.sum(row_exp, axis=1, keepdims=True)).astype(jnp.bfloat16)
    context = jnp.dot(attn_probs, value_rows, preferred_element_type=jnp.float32)
    return lax.all_to_all(context, "tp", split_axis=0, concat_axis=1, tiled=True)


def solution(mesh):
    placed = (P("grp", None), P("tp", "grp", None), P(), P("grp", None))
    return jax.shard_map(
        on_device, mesh=mesh, in_specs=placed, out_specs=P(("grp", "tp"), None), check_vma=False
    )
```

profile of v0, /device:TPU:1, one launch (start us, length us, event | category | flops | bytes accessed | tf_op | source)
XLA Modules:
  0.0 502.2 jit_solution(18027963017694480111)
XLA Ops:
  6.5 0.0 copy-start
  6.5 0.0 copy-start.1
  6.6 0.1 copy.31
  6.7 0.1 reshape.305
  6.8 0.4 copy-done.1
  7.2 1.2 gather_fusion
  8.5 0.1 min.12
  8.6 0.1 copy.32
  8.7 0.1 copy.35
  8.8 0.1 reshape.313
  8.9 0.1 reshape.339
  9.0 0.0 copy-done
  9.0 6.4 %gather_fusion.1 = bf16[96,320,128]{2,1,0:T(8,128)(2,1)} fusion(bf16[2,320,128]{2,1,0:T(8,128)(2,1)S(1)} %copy-done, s32[1024]{0:T(1024)S(1)} %pad_clamp_fusion.1), kind=kCustom, calls=%fused_computation.1 | custom fusion | bytes 15729024 | tf_op jit(solution)/shard_map/gather | solution.py:30
  15.4 6.9 %broadcast_select_fusion = bf16[32,3,320,128]{3,2,1,0:T(8,128)(2,1)} fusion(bf16[32,3,320,128]{3,2,1,0:T(8,128)(2,1)} %bitcast.34, pred[32,3]{1,0:T(8,128)(4,1)S(1)} %reshape.339), kind=kLoop, calls=%fused_computation.3 | loop fusion | flops 3932160 | bytes 15728736 | tf_op jit(solution)/shard_map/jit(_where)/select_n | solution.py:31
  22.3 0.0 copy-start.2
  22.3 17.1 %all-to-all-start = ((bf16[32,3,320,128]{3,2,1,0:T(8,128)(2,1)}), bf16[32,3,320,128]{3,2,1,0:T(8,128)(2,1)}, u32[]{:S(2)}, u32[]{:S(2)}) async-start(bf16[32,3,320,128]{3,2,1,0:T(8,128)(2,1)} %broadcast_select_fusion), calls=%async_computation | async-start | bytes 15728640 | tf_op jit(solution)/shard_map/all_to_all | solution.py:32
  39.4 0.0 all-gather.2.cloned.1.call-start
  39.5 0.1 fusion.8
  39.6 0.6 gather_fusion.2
  40.2 0.7 fusion.9
  46.5 332.2 %all-to-all-done = bf16[32,3,320,128]{3,2,1,0:T(8,128)(2,1)} async-done(((bf16[32,3,320,128]{3,2,1,0:T(8,128)(2,1)}), bf16[32,3,320,128]{3,2,1,0:T(8,128)(2,1)}, u32[]{:S(2)}, u32[]{:S(2)}) %all-to-all-start) | async-done | bytes 7864352 | tf_op jit(solution)/shard_map/all_to_all | solution.py:32
  378.6 1.0 dynamic-slice_bitcast_fusion.2
  379.6 0.7 pad_maximum_fusion
  380.3 0.0 all-gather.2.cloned.1.call-update
  380.4 0.0 copy-done.2
  380.4 0.2 reduce-window.8
  380.6 0.1 convert_reduce_fusion
  380.7 66.1 %all-gather.2.cloned.1.call-done = bf16[5120,3,128]{2,0,1:T(8,128)(2,1)} async-done(((bf16[320,3,128]{2,0,1:T(8,128)(2,1)}), bf16[5120,3,128]{2,0,1:T(8,128)(2,1)}) %all-gather.2.cloned.1.call-update) | async-done | bytes 3932176 | tf_op jit(solution)/shard_map/all_gather | solution.py:35
  446.8 6.3 %copy.36 = bf16[5120,3,128]{0,2,1:T(8,128)(2,1)} copy(bf16[5120,3,128]{2,0,1:T(8,128)(2,1)} %all-gather.2.cloned.1.call-done) | data formatting | bytes 7864320 | tf_op jit(solution)/shard_map/all_gather | solution.py:35
  453.1 5.5 %fusion.1 = bf16[384,384]{0,1:T(8,128)(2,1)S(1)} fusion(bf16[5120,384]{0,1:T(8,128)(2,1)} %bitcast.35, bf16[384,5120]{1,0:T(8,128)(2,1)} %param.4), kind=kOutput, calls=%fused_computation.7 | convolution fusion | flops 1510096896 | bytes 8159232 | tf_op jit(solution)/shard_map/dot_general | solution.py:37
  458.6 0.3 fusion.10
  458.9 0.1 fusion.3
  459.1 0.3 fusion.4
  459.4 35.0 %all_to_all.24 = f32[32,12,128]{2,1,0:T(8,128)S(1)} all-to-all(f32[32,12,128]{2,1,0:T(8,128)S(1)} %all_to_all.18), channel_id=1, replica_groups=mesh['grp'=16,'tp'=32] {'tp'}, dimensions={0} | all-to-all | bytes 393216 | tf_op jit(solution)/shard_map/all_to_all | solution.py:58
  494.4 0.1 copy.37
  494.5 0.9 copy.38
  (12 shorter events, 0.1 us)
Async XLA Ops:
  6.5 2.5 copy-start
  6.5 0.7 copy-start.1
  22.3 358.1 %copy-start.2 = (s32[1,4]{1,0:T(1,128)S(1)}, s32[1,4]{1,0:T(1,128)}, u32[]{:S(2)}) copy-start(s32[1,4]{1,0:T(1,128)} %param.7) | copy-start | bytes 52
  22.3 356.3 %all-to-all-start = ((bf16[32,3,320,128]{3,2,1,0:T(8,128)(2,1)}), bf16[32,3,320,128]{3,2,1,0:T(8,128)(2,1)}, u32[]{:S(2)}, u32[]{:S(2)}) async-start(bf16[32,3,320,128]{3,2,1,0:T(8,128)(2,1)} %broadcast_select_fusion), calls=%async_computation | async-start | bytes 15728640 | tf_op jit(solution)/shard_map/all_to_all | solution.py:32
  39.4 407.3 %all-gather.2.cloned.1.call-start = ((), (), s32[]{:S(2)}) async-start(), calls=%async_computation.2 | async-start | bytes 4177920 | tf_op jit(solution)/shard_map/all_gather | solution.py:35
Sparse Core Ops, SparseCore 0:
  380.5 66.2 all-gather.1
where the time goes:
time: 503 us; the launch traced here: 502 us
  waiting for transfers between devices  398 us (79%)
  blocking collectives  35 us (7%)
  between operations  19.1 us (4%)
  local copies, waits for them, and re-layouts  18.3 us (4%)
  starting transfers between devices  17.2 us (3%)
  other arithmetic  8.16 us (2%)
  matrix products  6.13 us (1%)
    all_to_all x1, waiting for transfers between devices, on_device(): lax.all_to_all(outbound, 'tp', split_axis=0, concat_axis=0, tiled=True)  332 us
    all_gather x1, waiting for transfers between devices, on_device(): full_panels = lax.all_gather(selected, 'grp', axis=0, tiled=True)  66.1 us
    all_to_all x1, blocking collectives, on_device(): lax.all_to_all(context, 'tp', split_axis=0, concat_axis=1, tiled=True)  35 us
    all_to_all x1, starting transfers between devices, on_device(): lax.all_to_all(outbound, 'tp', split_axis=0, concat_axis=0, tiled=True)  17.1 us
  transfers between devices with their start and end apart: 2, of which 2 were waited for; matrix products, arithmetic and copies ran while one was open for 0% of the time, Pallas kernels for 0%

commit v1 on v0

--- a/solution.py
+++ b/solution.py
@@ -2,6 +2,29 @@
 import jax.numpy as jnp
 from jax import lax
 from jax.sharding import PartitionSpec as P
+
+
+def vector_supply_all(mat):
+    w2 = lax.axis_size("grp")
+    q_next = lax.axis_index("grp")
+    e_now, block_last, response = (w2, q_next, mat.shape[0])
+    pile = [(s, (s + 1) % e_now) for s in range(e_now)]
+    panels = [(s, (s - 1) % e_now) for s in range(e_now)]
+    front = jnp.zeros((*mat.shape[:0], e_now * response, *mat.shape[1:]), mat.dtype)
+    front = lax.dynamic_update_slice_in_dim(front, mat, block_last * response, axis=0)
+    res = raw_out = mat
+    f_next = e_now // 2
+    for w in [*range(1, f_next + 1)]:
+        res = lax.ppermute(res, perm=pile, axis_name="grp")
+        front = lax.dynamic_update_slice_in_dim(
+            front, res, (block_last - w) % e_now * response, axis=0
+        )
+        if w < e_now - f_next:
+            raw_out = lax.ppermute(raw_out, axis_name="grp", perm=panels)
+            front = lax.dynamic_update_slice_in_dim(
+                front, raw_out, (block_last + w) % e_now * response, axis=0
+            )
+    return front
 
 
 def on_device(tokens, trainer_panels, panel_home, lengths):
@@ -32,7 +55,7 @@
     arrived = lax.all_to_all(outbound, "tp", split_axis=0, concat_axis=0, tiled=True)
     source = wanted // slot_count
     selected = jnp.stack([arrived[source[need_pos], need_pos] for need_pos in range(3)], axis=1)
-    full_panels = lax.all_gather(selected, "grp", axis=0, tiled=True)
+    full_panels = vector_supply_all(selected)
     weights = full_panels.reshape(full_panels.shape[0], 3 * head_dim)
     projected = jnp.dot(tokens, weights, preferred_element_type=jnp.float32).astype(jnp.bfloat16)
     query_rows = projected[:, :head_dim]

time: 503 us -> 570 us (1.13)
  starting transfers between devices: 17.2 us -> 79.6 us
  local copies, waits for them, and re-layouts: 18.3 us -> 73.8 us
  waiting for transfers between devices: 398 us -> 352 us
  between operations: 19.1 us -> 6.31 us
  blocking collectives: 35 us -> 42.4 us
    all_gather x1 -> x0, waiting for transfers between devices: 66.1 us -> none  [on_device(): full_panels = lax.all_gather(selected, 'grp', axis=0, tiled=True)]
    ppermute x0 -> x15, starting transfers between devices: none -> 62.5 us  [the longest x7 45.8 us: vector_supply_all(): raw_out = lax.ppermute(raw_out, axis_name='grp', perm=panels)]
    dynamic_update_slice x0 -> x16, local copies, waits for them, and re-layouts: none -> 59.1 us  [the longest x8 29.2 us: vector_supply_all(): lax.dynamic_update_slice_in_dim(front, res, (block_last - w) % e_now * re...]
    ppermute x0 -> x15, waiting for transfers between devices: none -> 20.3 us  [the longest x8 20.3 us: vector_supply_all(): res = lax.ppermute(res, perm=pile, axis_name='grp')]
    all_to_all x1, blocking collectives: 35 us -> 42.4 us  [on_device(): lax.all_to_all(context, 'tp', split_axis=0, concat_axis=1, tiled=True)]
    all_gather x1 -> x0, local copies, waits for them, and re-layouts: 6.33 us -> none  [on_device(): full_panels = lax.all_gather(selected, 'grp', axis=0, tiled=True)]
  transfers between devices with their start and end apart: 2 -> 16, of which waited for: 2 -> 8; matrix products, arithmetic and copies ran while one was open for 0% -> 10% of each run, Pallas kernels for 0% -> 0%
where the time goes in v1:
time: 570 us; the launch traced here: 568 us
  waiting for transfers between devices  352 us (62%)
  starting transfers between devices  79.6 us (14%)
  local copies, waits for them, and re-layouts  73.8 us (13%)
  blocking collectives  42.4 us (7%)
  other arithmetic  7.49 us (1%)
  between operations  6.31 us (1%)
  matrix products  6.13 us (1%)
    all_to_all x1, waiting for transfers between devices, on_device(): lax.all_to_all(outbound, 'tp', split_axis=0, concat_axis=0, tiled=True)  332 us
    ppermute x7, starting transfers between devices, vector_supply_all(): raw_out = lax.ppermute(raw_out, axis_name='grp', perm=panels)  45.8 us
    all_to_all x1, blocking collectives, on_device(): lax.all_to_all(context, 'tp', split_axis=0, concat_axis=1, tiled=True)  42.4 us
    dynamic_update_slice x8, local copies, waits for them, and re-layouts, vector_supply_all(): lax.dynamic_update_slice_in_dim(front, res, (block_last - w) % e_now * re...  29.2 us
    dynamic_update_slice x7, local copies, waits for them, and re-layouts, vector_supply_all(): lax.dynamic_update_slice_in_dim(front, raw_out, (block_last + w) % e_now...  26.5 us
    ppermute x8, waiting for transfers between devices, vector_supply_all(): res = lax.ppermute(res, perm=pile, axis_name='grp')  20.3 us
    all_to_all x1, starting transfers between devices, on_device(): lax.all_to_all(outbound, 'tp', split_axis=0, concat_axis=0, tiled=True)  17.1 us
    ppermute x8, starting transfers between devices, vector_supply_all(): res = lax.ppermute(res, perm=pile, axis_name='grp')  16.7 us
  transfers between devices with their start and end apart: 16, of which 8 were waited for; matrix products, arithmetic and copies ran while one was open for 10% of the time, Pallas kernels for 0%

profile of v1, /device:TPU:1, one launch (start us, length us, event | category | flops | bytes accessed | tf_op | source)
XLA Modules:
  0.0 568.2 jit_solution(1132833725522814117)
XLA Ops:
  0.0 0.1 copy.33
  0.1 0.1 reshape.305
  0.3 0.4 copy-done.1
  0.7 1.2 gather_fusion
  2.0 0.1 min.12
  2.1 0.1 copy.37
  2.2 0.1 reshape.313
  2.4 0.1 reshape.339
  2.5 6.4 %gather_fusion.1 = bf16[96,320,128]{2,1,0:T(8,128)(2,1)} fusion(bf16[2,320,128]{2,1,0:T(8,128)(2,1)S(1)} %copy-done, s32[1024]{0:T(1024)S(1)} %pad_clamp_fusion.1), kind=kCustom, calls=%fused_computation.1 | custom fusion | bytes 15729024 | tf_op jit(solution)/shard_map/gather | solution.py:53
  8.9 6.9 %broadcast_select_fusion = bf16[32,3,320,128]{3,2,1,0:T(8,128)(2,1)} fusion(bf16[32,3,320,128]{3,2,1,0:T(8,128)(2,1)} %bitcast.31, pred[32,3]{1,0:T(8,128)(4,1)S(1)} %reshape.339), kind=kLoop, calls=%fused_computation.3 | loop fusion | flops 3932160 | bytes 15728736 | tf_op jit(solution)/shard_map/jit(_where)/select_n | solution.py:54
  15.8 17.1 %all-to-all-start = ((bf16[32,3,320,128]{3,2,1,0:T(8,128)(2,1)}), bf16[32,3,320,128]{3,2,1,0:T(8,128)(2,1)}, u32[]{:S(2)}, u32[]{:S(2)}) async-start(bf16[32,3,320,128]{3,2,1,0:T(8,128)(2,1)} %broadcast_select_fusion), calls=%async_computation | async-start | bytes 15728640 | tf_op jit(solution)/shard_map/all_to_all | solution.py:55
  33.0 0.6 gather_fusion.2
  33.7 0.6 fusion.9
  39.9 332.2 %all-to-all-done = bf16[32,3,320,128]{3,2,1,0:T(8,128)(2,1)} async-done(((bf16[32,3,320,128]{3,2,1,0:T(8,128)(2,1)}), bf16[32,3,320,128]{3,2,1,0:T(8,128)(2,1)}, u32[]{:S(2)}, u32[]{:S(2)}) %all-to-all-start) | async-done | bytes 7864352 | tf_op jit(solution)/shard_map/all_to_all | solution.py:55
  372.1 1.0 constant_dynamic-slice_fusion.2
  373.1 0.1 copy.38
  373.2 0.1 copy.39
  373.3 0.1 copy.40
  373.5 3.1 collective-permute-start
  376.7 5.6 collective-permute-start.1
  382.3 4.8 collective-permute-done
  387.1 1.9 collective-permute-start.2
  389.1 6.7 %collective-permute-start.3 = (bf16[320,3,128]{0,2,1:T(8,128)(2,1)S(1)}, bf16[320,3,128]{0,2,1:T(8,128)(2,1)S(1)}, u32[]{:S(2)}, u32[]{:S(2)}) collective-permute-start(bf16[320,3,128]{0,2,1:T(8,128)(2,1)S(1)} %collective-permute-done.1), channel_id=1, source_target_pairs={{0,480},{32,0},{64,32},{96,64},{128,96},{160,128},{192,160},{224,1... | collective-permute-start | bytes 737288 | tf_op jit(solution)/shard_map/ppermute | solution.py:23
  395.7 3.9 collective-permute-done.2
  399.6 1.9 collective-permute-start.4
  401.5 6.7 %collective-permute-start.5 = (bf16[320,3,128]{0,2,1:T(8,128)(2,1)S(1)}, bf16[320,3,128]{0,2,1:T(8,128)(2,1)S(1)}, u32[]{:S(2)}, u32[]{:S(2)}) collective-permute-start(bf16[320,3,128]{0,2,1:T(8,128)(2,1)S(1)} %collective-permute-done.3), channel_id=1, source_target_pairs={{0,480},{32,0},{64,32},{96,64},{128,96},{160,128},{192,160},{224,1... | collective-permute-start | bytes 737288 | tf_op jit(solution)/shard_map/ppermute | solution.py:23
  408.2 3.0 collective-permute-done.4
  411.2 1.9 collective-permute-start.6
  413.1 6.7 %collective-permute-start.7 = (bf16[320,3,128]{0,2,1:T(8,128)(2,1)S(1)}, bf16[320,3,128]{0,2,1:T(8,128)(2,1)S(1)}, u32[]{:S(2)}, u32[]{:S(2)}) collective-permute-start(bf16[320,3,128]{0,2,1:T(8,128)(2,1)S(1)} %collective-permute-done.5), channel_id=1, source_target_pairs={{0,480},{32,0},{64,32},{96,64},{128,96},{160,128},{192,160},{224,1... | collective-permute-start | bytes 737288 | tf_op jit(solution)/shard_map/ppermute | solution.py:23
  419.8 2.2 collective-permute-done.6
  422.0 1.9 collective-permute-start.8
  423.9 6.7 %collective-permute-start.9 = (bf16[320,3,128]{0,2,1:T(8,128)(2,1)S(1)}, bf16[320,3,128]{0,2,1:T(8,128)(2,1)S(1)}, u32[]{:S(2)}, u32[]{:S(2)}) collective-permute-start(bf16[320,3,128]{0,2,1:T(8,128)(2,1)S(1)} %collective-permute-done.7), channel_id=1, source_target_pairs={{0,480},{32,0},{64,32},{96,64},{128,96},{160,128},{192,160},{224,1... | collective-permute-start | bytes 737288 | tf_op jit(solution)/shard_map/ppermute | solution.py:23
  430.6 2.2 collective-permute-done.8
  432.7 1.9 collective-permute-start.10
  434.7 6.7 %collective-permute-start.11 = (bf16[320,3,128]{0,2,1:T(8,128)(2,1)S(1)}, bf16[320,3,128]{0,2,1:T(8,128)(2,1)}, u32[]{:S(2)}, u32[]{:S(2)}) collective-permute-start(bf16[320,3,128]{0,2,1:T(8,128)(2,1)S(1)} %collective-permute-done.9), channel_id=1, source_target_pairs={{0,480},{32,0},{64,32},{96,64},{128,96},{160,128},{192,160},{224,1... | collective-permute-start | bytes 737288 | tf_op jit(solution)/shard_map/ppermute | solution.py:23
  441.4 2.2 collective-permute-done.10
  443.5 1.9 collective-permute-start.12
  445.5 6.8 %collective-permute-start.13 = (bf16[320,3,128]{0,2,1:T(8,128)(2,1)}, bf16[320,3,128]{0,2,1:T(8,128)(2,1)}, u32[]{:S(2)}, u32[]{:S(2)}) collective-permute-start(bf16[320,3,128]{0,2,1:T(8,128)(2,1)} %collective-permute-done.11), channel_id=1, source_target_pairs={{0,480},{32,0},{64,32},{96,64},{128,96},{160,128},{192,160},{224,1... | collective-permute-start | bytes 737288 | tf_op jit(solution)/shard_map/ppermute | solution.py:23
  452.2 2.2 collective-permute-done.12
  454.4 2.1 collective-permute-start.14
  456.8 0.2 reduce-window.8
  457.1 2.3 broadcast_in_dim.15
  459.4 3.5 dynamic_update_slice.48
  462.9 3.3 dynamic_update_slice.49
  466.2 4.0 dynamic_update_slice.50
  470.1 3.4 dynamic_update_slice.51
  473.5 3.5 dynamic_update_slice.52
  477.1 4.0 dynamic_update_slice.53
  481.0 4.0 dynamic_update_slice.54
  485.0 3.5 dynamic_update_slice.55
  488.5 3.5 dynamic_update_slice.56
  492.0 4.0 dynamic_update_slice.57
  496.0 4.0 dynamic_update_slice.58
  499.9 3.5 dynamic_update_slice.59
  503.4 3.6 dynamic_update_slice.60
  506.9 4.0 dynamic_update_slice.61
  510.9 4.0 dynamic_update_slice.62
  514.9 3.6 dynamic_update_slice.63
  518.5 5.5 fusion.1
  524.1 0.3 fusion.10
  524.4 0.1 fusion.3
  524.5 0.3 fusion.4
  524.8 42.4 %all_to_all.24 = f32[32,12,128]{2,1,0:T(8,128)S(1)} all-to-all(f32[32,12,128]{2,1,0:T(8,128)S(1)} %all_to_all.18), channel_id=1, replica_groups=mesh['grp'=16,'tp'=32] {'tp'}, dimensions={0} | all-to-all | bytes 393216 | tf_op jit(solution)/shard_map/all_to_all | solution.py:81
  567.3 0.9 copy.42
  (34 shorter events, 0.5 us)
Async XLA Ops:
  0.0 2.5 copy-start
  0.0 0.7 copy-start.1
  15.8 441.0 %copy-start.4 = (s32[1,4]{1,0:T(1,128)S(1)}, s32[1,4]{1,0:T(1,128)}, u32[]{:S(2)}) copy-start(s32[1,4]{1,0:T(1,128)} %param.7) | copy-start | bytes 52
  15.8 356.3 %all-to-all-start = ((bf16[32,3,320,128]{3,2,1,0:T(8,128)(2,1)}), bf16[32,3,320,128]{3,2,1,0:T(8,128)(2,1)}, u32[]{:S(2)}, u32[]{:S(2)}) async-start(bf16[32,3,320,128]{3,2,1,0:T(8,128)(2,1)} %broadcast_select_fusion), calls=%async_computation | async-start | bytes 15728640 | tf_op jit(solution)/shard_map/all_to_all | solution.py:55
  373.5 13.6 %collective-permute-start = (bf16[320,3,128]{0,2,1:T(8,128)(2,1)S(1)}, bf16[320,3,128]{0,2,1:T(8,128)(2,1)S(1)}, u32[]{:S(2)}, u32[]{:S(2)}) collective-permute-start(bf16[320,3,128]{0,2,1:T(8,128)(2,1)S(1)} %pad_maximum_fusion), channel_id=1, source_target_pairs={{0,32},{32,64},{64,96},{96,128},{128,160},{160,192},{192,224},{224... | collective-permute-start | bytes 737288 | tf_op jit(solution)/shard_map/ppermute | solution.py:18
  376.7 12.4 %collective-permute-start.1 = (bf16[320,3,128]{0,2,1:T(8,128)(2,1)S(1)}, bf16[320,3,128]{0,2,1:T(8,128)(2,1)S(1)}, u32[]{:S(2)}, u32[]{:S(2)}) collective-permute-start(bf16[320,3,128]{0,2,1:T(8,128)(2,1)S(1)} %pad_maximum_fusion), channel_id=1, source_target_pairs={{0,480},{32,0},{64,32},{96,64},{128,96},{160,128},{192,160},{224,1... | collective-permute-start | bytes 737288 | tf_op jit(solution)/shard_map/ppermute | solution.py:23
  387.1 12.5 %collective-permute-start.2 = (bf16[320,3,128]{0,2,1:T(8,128)(2,1)S(1)}, bf16[320,3,128]{0,2,1:T(8,128)(2,1)S(1)}, u32[]{:S(2)}, u32[]{:S(2)}) collective-permute-start(bf16[320,3,128]{0,2,1:T(8,128)(2,1)S(1)} %collective-permute-done), channel_id=1, source_target_pairs={{0,32},{32,64},{64,96},{96,128},{128,160},{160,192},{192,224},{224... | collective-permute-start | bytes 737288 | tf_op jit(solution)/shard_map/ppermute | solution.py:18
  389.1 12.5 %collective-permute-start.3 = (bf16[320,3,128]{0,2,1:T(8,128)(2,1)S(1)}, bf16[320,3,128]{0,2,1:T(8,128)(2,1)S(1)}, u32[]{:S(2)}, u32[]{:S(2)}) collective-permute-start(bf16[320,3,128]{0,2,1:T(8,128)(2,1)S(1)} %collective-permute-done.1), channel_id=1, source_target_pairs={{0,480},{32,0},{64,32},{96,64},{128,96},{160,128},{192,160},{224,1... | collective-permute-start | bytes 737288 | tf_op jit(solution)/shard_map/ppermute | solution.py:23
  399.6 11.6 %collective-permute-start.4 = (bf16[320,3,128]{0,2,1:T(8,128)(2,1)S(1)}, bf16[320,3,128]{0,2,1:T(8,128)(2,1)S(1)}, u32[]{:S(2)}, u32[]{:S(2)}) collective-permute-start(bf16[320,3,128]{0,2,1:T(8,128)(2,1)S(1)} %collective-permute-done.2), channel_id=1, source_target_pairs={{0,32},{32,64},{64,96},{96,128},{128,160},{160,192},{192,224},{224... | collective-permute-start | bytes 737288 | tf_op jit(solution)/shard_map/ppermute | solution.py:18
  401.5 11.6 %collective-permute-start.5 = (bf16[320,3,128]{0,2,1:T(8,128)(2,1)S(1)}, bf16[320,3,128]{0,2,1:T(8,128)(2,1)S(1)}, u32[]{:S(2)}, u32[]{:S(2)}) collective-permute-start(bf16[320,3,128]{0,2,1:T(8,128)(2,1)S(1)} %collective-permute-done.3), channel_id=1, source_target_pairs={{0,480},{32,0},{64,32},{96,64},{128,96},{160,128},{192,160},{224,1... | collective-permute-start | bytes 737288 | tf_op jit(solution)/shard_map/ppermute | solution.py:23
  411.2 10.8 %collective-permute-start.6 = (bf16[320,3,128]{0,2,1:T(8,128)(2,1)S(1)}, bf16[320,3,128]{0,2,1:T(8,128)(2,1)S(1)}, u32[]{:S(2)}, u32[]{:S(2)}) collective-permute-start(bf16[320,3,128]{0,2,1:T(8,128)(2,1)S(1)} %collective-permute-done.4), channel_id=1, source_target_pairs={{0,32},{32,64},{64,96},{96,128},{128,160},{160,192},{192,224},{224... | collective-permute-start | bytes 737288 | tf_op jit(solution)/shard_map/ppermute | solution.py:18
  413.1 10.8 %collective-permute-start.7 = (bf16[320,3,128]{0,2,1:T(8,128)(2,1)S(1)}, bf16[320,3,128]{0,2,1:T(8,128)(2,1)S(1)}, u32[]{:S(2)}, u32[]{:S(2)}) collective-permute-start(bf16[320,3,128]{0,2,1:T(8,128)(2,1)S(1)} %collective-permute-done.5), channel_id=1, source_target_pairs={{0,480},{32,0},{64,32},{96,64},{128,96},{160,128},{192,160},{224,1... | collective-permute-start | bytes 737288 | tf_op jit(solution)/shard_map/ppermute | solution.py:23
  422.0 10.8 %collective-permute-start.8 = (bf16[320,3,128]{0,2,1:T(8,128)(2,1)S(1)}, bf16[320,3,128]{0,2,1:T(8,128)(2,1)S(1)}, u32[]{:S(2)}, u32[]{:S(2)}) collective-permute-start(bf16[320,3,128]{0,2,1:T(8,128)(2,1)S(1)} %collective-permute-done.6), channel_id=1, source_target_pairs={{0,32},{32,64},{64,96},{96,128},{128,160},{160,192},{192,224},{224... | collective-permute-start | bytes 737288 | tf_op jit(solution)/shard_map/ppermute | solution.py:18
  423.9 10.8 %collective-permute-start.9 = (bf16[320,3,128]{0,2,1:T(8,128)(2,1)S(1)}, bf16[320,3,128]{0,2,1:T(8,128)(2,1)S(1)}, u32[]{:S(2)}, u32[]{:S(2)}) collective-permute-start(bf16[320,3,128]{0,2,1:T(8,128)(2,1)S(1)} %collective-permute-done.7), channel_id=1, source_target_pairs={{0,480},{32,0},{64,32},{96,64},{128,96},{160,128},{192,160},{224,1... | collective-permute-start | bytes 737288 | tf_op jit(solution)/shard_map/ppermute | solution.py:23
  432.7 10.8 %collective-permute-start.10 = (bf16[320,3,128]{0,2,1:T(8,128)(2,1)S(1)}, bf16[320,3,128]{0,2,1:T(8,128)(2,1)S(1)}, u32[]{:S(2)}, u32[]{:S(2)}) collective-permute-start(bf16[320,3,128]{0,2,1:T(8,128)(2,1)S(1)} %collective-permute-done.8), channel_id=1, source_target_pairs={{0,32},{32,64},{64,96},{96,128},{128,160},{160,192},{192,224},{224... | collective-permute-start | bytes 737288 | tf_op jit(solution)/shard_map/ppermute | solution.py:18
  434.7 10.8 %collective-permute-start.11 = (bf16[320,3,128]{0,2,1:T(8,128)(2,1)S(1)}, bf16[320,3,128]{0,2,1:T(8,128)(2,1)}, u32[]{:S(2)}, u32[]{:S(2)}) collective-permute-start(bf16[320,3,128]{0,2,1:T(8,128)(2,1)S(1)} %collective-permute-done.9), channel_id=1, source_target_pairs={{0,480},{32,0},{64,32},{96,64},{128,96},{160,128},{192,160},{224,1... | collective-permute-start | bytes 737288 | tf_op jit(solution)/shard_map/ppermute | solution.py:23
  443.5 1.9 copy-start.2
  443.5 10.9 %collective-permute-start.12 = (bf16[320,3,128]{0,2,1:T(8,128)(2,1)S(1)}, bf16[320,3,128]{0,2,1:T(8,128)(2,1)}, u32[]{:S(2)}, u32[]{:S(2)}) collective-permute-start(bf16[320,3,128]{0,2,1:T(8,128)(2,1)S(1)} %collective-permute-done.10), channel_id=1, source_target_pairs={{0,32},{32,64},{64,96},{96,128},{128,160},{160,192},{192,224},{224... | collective-permute-start | bytes 737288 | tf_op jit(solution)/shard_map/ppermute | solution.py:18
  445.5 65.4 %collective-permute-start.13 = (bf16[320,3,128]{0,2,1:T(8,128)(2,1)}, bf16[320,3,128]{0,2,1:T(8,128)(2,1)}, u32[]{:S(2)}, u32[]{:S(2)}) collective-permute-start(bf16[320,3,128]{0,2,1:T(8,128)(2,1)} %collective-permute-done.11), channel_id=1, source_target_pairs={{0,480},{32,0},{64,32},{96,64},{128,96},{160,128},{192,160},{224,1... | collective-permute-start | bytes 737288 | tf_op jit(solution)/shard_map/ppermute | solution.py:23
  454.4 60.5 %collective-permute-start.14 = (bf16[320,3,128]{0,2,1:T(8,128)(2,1)}, bf16[320,3,128]{0,2,1:T(8,128)(2,1)}, u32[]{:S(2)}, u32[]{:S(2)}) collective-permute-start(bf16[320,3,128]{0,2,1:T(8,128)(2,1)} %collective-permute-done.12), channel_id=1, source_target_pairs={{0,32},{32,64},{64,96},{96,128},{128,160},{160,192},{192,224},{224... | collective-permute-start | bytes 737288 | tf_op jit(solution)/shard_map/ppermute | solution.py:18
  462.9 37.1 %copy-start.3 = (bf16[320,3,128]{0,2,1:T(8,128)(2,1)S(1)}, bf16[320,3,128]{0,2,1:T(8,128)(2,1)}, u32[]{:S(2)}) copy-start(bf16[320,3,128]{0,2,1:T(8,128)(2,1)} %copy-done.2) | copy-start | bytes 737284
